TPU v7x, 32 devices: a whole 2x2x4 slice. The times are simulated.
32 devices in a mesh: aa: 4 (over z), ba: 8 (over y, x, core).
Axes of the slice: x: 2, y: 2, z: 4, core: 2. Of those that a mesh axis runs over, the one named last changes fastest.
Arguments:
- feats: bfloat16 [4, 32, 128, 256], P('aa', 'ba'), may hold values from -6 to 6
- conv_one: bfloat16 [3, 3, 3, 256, 256], replicated, may hold values from -0.078125 to 0.078125
- bias_one: float32 [256], replicated, may hold values from -3 to 3
- conv_two: bfloat16 [3, 3, 3, 256, 256], replicated, may hold values from -0.078125 to 0.078125
- bias_two: float32 [256], replicated, may hold values from -3 to 3
- patch_weight: bfloat16 [2, 2, 256, 128], replicated, may hold values from -0.1875 to 0.1875
- patch_bias: float32 [128], replicated, may hold values from -3 to 3
- embed_weight: bfloat16 [128, 2048], replicated, may hold values from -0.5 to 0.5
- embed_bias: float32 [2048], replicated, may hold values from -6 to 6
- norm_gain: float32 [2048], replicated, may hold values from 0.1 to 1.9
- w_query: bfloat16 [2048, 2048], P(None, 'ba'), may hold values from -2 to 2
- w_key: bfloat16 [2048, 2048], P(None, 'ba'), may hold values from -2 to 2
- w_value: bfloat16 [2048, 2048], P(None, 'ba'), may hold values from -0.125 to 0.125
- w_velocity: bfloat16 [2048, 128], P('ba'), may hold values from -0.5 to 0.5
Outputs:
- velocity: float32 [4096, 128], P(('aa', 'ba'))
All inputs are finite; a program needn't handle non-finite values.
Results may differ from a plain program's by a relative error of at most 0.035.
Values may be sent and summed in bfloat16 or wider, within the bound.
A program may use at most 128 MiB of HBM per device.

v0:
```python
import math
import jax
import jax.numpy as jnp
from jax import lax
from jax.sharding import PartitionSpec as P

HEAD_DIM = 64


def with_halo(cells, sides, width):
    for axis, dim in sides:
        count = lax.axis_size(axis)
        ends = count - 1
        head = lax.slice_in_dim(cells, 0, width, axis=dim)
        tail = lax.slice_in_dim(cells, cells.shape[dim] - width, cells.shape[dim], axis=dim)
        cells = jnp.concatenate(
            [
                lax.ppermute(tail, axis, [(i, (i + 1) % count) for i in range(ends)]),
                cells,
                lax.ppermute(head, axis, [((i + 1) % count, i) for i in range(ends)]),
            ],
            axis=dim,
        )
    return cells


def convolve(field, kernel, bias):
    frames, rows, width, chans = field.shape
    padded = with_halo(field, (("aa", 0), ("ba", 1)), 1)
    padded = jnp.pad(padded, ((0, 0), (0, 0), (1, 1), (0, 0)))
    total = jnp.zeros((frames * rows * width, kernel.shape[-1]), jnp.float32)
    for shift_t in range(3):
        for shift_r in range(3):
            window = padded[shift_t : shift_t + frames, shift_r : shift_r + rows]
            stacked = jnp.concatenate(
                [window[:, :, shift_w : shift_w + width] for shift_w in range(3)], axis=-1
            )
            total = total + jnp.dot(
                stacked.reshape(-1, 3 * chans),
                kernel[shift_t, shift_r].reshape(3 * chans, -1),
                preferred_element_type=jnp.float32,
            )
    return (total + bias).reshape(frames, rows, width, -1)


def patchify(field, weight, bias):
    frames, rows, width, chans = field.shape
    blocks = (
        field.reshape(frames, rows // 2, 2, width // 2, 2, chans)
        .transpose(0, 1, 3, 2, 4, 5)
        .reshape(-1, 4 * chans)
    )
    return (
        jnp.dot(blocks, weight.reshape(4 * chans, -1), preferred_element_type=jnp.float32) + bias
    ).astype(jnp.bfloat16)


def normalize(latent_rows, embed_weight, embed_bias, norm_gain):
    hidden = jnp.dot(latent_rows, embed_weight, preferred_element_type=jnp.float32) + embed_bias
    center = hidden - hidden.mean(-1, keepdims=True)
    spread = (center * center).mean(-1, keepdims=True)
    return (center * lax.rsqrt(spread + 1e-05) * norm_gain).astype(jnp.bfloat16)


def attend(queries, keys, values):
    rows, width = queries.shape
    heads = width // HEAD_DIM
    scale = HEAD_DIM ** (-0.5)
    query_heads = queries.reshape(rows, heads, HEAD_DIM)
    start_state = (
        jnp.full((heads, rows), -jnp.inf, jnp.float32),
        jnp.zeros((heads, rows), jnp.float32),
        jnp.zeros((rows, heads, HEAD_DIM), jnp.float32),
    )
    key_rows = lax.all_gather(keys, "aa", axis=0, tiled=True)
    value_rows = lax.all_gather(values, "aa", axis=0, tiled=True)
    count = key_rows.shape[0]
    block = math.gcd(count, 1024)

    def one_step(index, state):
        best, denom, accum = state
        key_block = lax.dynamic_slice_in_dim(key_rows, index * block, block, 0).reshape(
            block, heads, HEAD_DIM
        )
        value_block = lax.dynamic_slice_in_dim(value_rows, index * block, block, 0).reshape(
            block, heads, HEAD_DIM
        )
        scores = (
            jnp.einsum("qhd,khd->hqk", query_heads, key_block, preferred_element_type=jnp.float32)
            * scale
        )
        peak = jnp.maximum(best, scores.max(-1))
        probs = jnp.exp(scores - peak[..., None])
        fade = jnp.exp(best - peak)
        denom = denom * fade + probs.sum(-1)
        accum = accum * fade.T[..., None] + jnp.einsum(
            "hqk,khd->qhd",
            probs.astype(jnp.bfloat16),
            value_block,
            preferred_element_type=jnp.float32,
        )
        return (peak, denom, accum)

    best, denom, accum = lax.fori_loop(0, count // block, one_step, start_state)
    return (accum / denom.T[..., None]).reshape(rows, width).astype(jnp.bfloat16)


def on_device(
    feats,
    conv_one,
    bias_one,
    conv_two,
    bias_two,
    patch_weight,
    patch_bias,
    embed_weight,
    embed_bias,
    norm_gain,
    w_query,
    w_key,
    w_value,
    w_velocity,
):
    first = jax.nn.gelu(convolve(feats, conv_one, bias_one), approximate=False).astype(jnp.bfloat16)
    second = (
        first.astype(jnp.float32)
        + jax.nn.gelu(convolve(first, conv_two, bias_two), approximate=False)
    ).astype(jnp.bfloat16)
    latents = patchify(second, patch_weight, patch_bias)
    width = w_query.shape[1]
    w_joined = jnp.concatenate([w_query, w_key, w_value], axis=1)
    joined = jnp.dot(
        normalize(
            lax.all_gather(latents, "ba", axis=0, tiled=True), embed_weight, embed_bias, norm_gain
        ),
        w_joined,
        preferred_element_type=jnp.float32,
    ).astype(jnp.bfloat16)
    attended = attend(joined[:, :width], joined[:, width : 2 * width], joined[:, 2 * width :])
    return lax.psum_scatter(
        jnp.dot(attended, w_velocity, preferred_element_type=jnp.float32).astype(jnp.bfloat16),
        "ba",
        scatter_dimension=0,
        tiled=True,
    ).astype(jnp.float32)


def solution(mesh):
    return jax.shard_map(
        on_device,
        mesh=mesh,
        in_specs=(
            P("aa", "ba", None, None),
            P(),
            P(),
            P(),
            P(),
            P(),
            P(),
            P(),
            P(),
            P(),
            P(None, "ba"),
            P(None, "ba"),
            P(None, "ba"),
            P("ba", None),
        ),
        out_specs=P(("aa", "ba"), None),
        check_vma=False,
    )
```

profile of v0, /device:TPU:0, one launch (start us, length us, event | category | flops | bytes accessed | tf_op | source)
XLA Modules:
  0.0 332.6 jit_solution(549942878547130094)
XLA Ops:
  6.5 5.1 %collective-permute-start = (bf16[1,4,128,256]{3,2,1,0:T(8,128)(2,1)}, bf16[1,4,128,256]{3,2,1,0:T(8,128)(2,1)S(1)}, u32[]{:S(2)}, u32[]{:S(2)}) collective-permute-start(bf16[1,4,128,256]{3,2,1,0:T(8,128)(2,1)} %param.16), channel_id=1, source_target_pairs={{0,8},{8,16},{16,24},{1,9},{9,17},{17,25},{2,10},{10,18},{18,26},{... | collective-permute-start | bytes 786440 | tf_op jit(solution)/shard_map/ppermute | solution.py:18
  12.9 4.5 %collective-permute-done = bf16[1,4,128,256]{3,2,1,0:T(8,128)(2,1)S(1)} collective-permute-done((bf16[1,4,128,256]{3,2,1,0:T(8,128)(2,1)}, bf16[1,4,128,256]{3,2,1,0:T(8,128)(2,1)S(1)}, u32[]{:S(2)}, u32[]{:S(2)}) %collective-permute-start) | collective-permute-done | bytes 262176 | tf_op jit(solution)/shard_map/ppermute | solution.py:18
  18.5 3.0 collective-permute-done.1
  24.2 2.2 fusion.102
  26.4 1.6 collective-permute-done.3
  33.6 2.1 fusion.69
  36.8 3.5 %collective-permute-start.4 = (bf16[1,4,128,256]{3,2,1,0:T(8,128)(2,1)S(1)}, bf16[1,4,128,256]{3,2,1,0:T(8,128)(2,1)S(1)}, u32[]{:S(2)}, u32[]{:S(2)}) collective-permute-start(bf16[1,4,128,256]{3,2,1,0:T(8,128)(2,1)S(1)} %fusion.66), channel_id=1, source_target_pairs={{0,8},{8,16},{16,24},{1,9},{9,17},{17,25},{2,10},{10,18},{18,26},{... | collective-permute-start | bytes 786440 | tf_op jit(solution)/shard_map/ppermute | solution.py:18
  41.6 2.6 collective-permute-done.4
  44.1 4.4 %collective-permute-done.5 = bf16[1,4,128,256]{3,2,1,0:T(8,128)(2,1)S(1)} collective-permute-done((bf16[1,4,128,256]{3,2,1,0:T(8,128)(2,1)S(1)}, bf16[1,4,128,256]{3,2,1,0:T(8,128)(2,1)S(1)}, u32[]{:S(2)}, u32[]{:S(2)}) %collective-permute-start.5) | collective-permute-done | bytes 262176 | tf_op jit(solution)/shard_map/ppermute | solution.py:20
  49.3 5.3 %collective-permute-start.6 = (bf16[3,1,128,256]{3,2,1,0:T(8,128)(2,1)}, bf16[3,1,128,256]{3,2,1,0:T(8,128)(2,1)}, u32[]{:S(2)}, u32[]{:S(2)}) collective-permute-start(bf16[3,1,128,256]{3,2,1,0:T(8,128)(2,1)} %get-tuple-element.246), channel_id=1, source_target_pairs={{0,1},{1,2},{2,3},{3,4},{4,5},{5,6},{6,7},{8,9},{9,10},{10,11},{11... | collective-permute-start | bytes 589832 | tf_op jit(solution)/shard_map/ppermute | solution.py:18
  54.6 1.5 collective-permute-start.7
  56.1 1.7 fusion.101
  59.6 1.5 select_maximum_fusion.1
  70.8 2.2 fusion.98
  74.7 15.0 %all_gather.9 = bf16[1024,128]{1,0:T(8,128)(2,1)S(1)} all-gather(bf16[128,128]{1,0:T(8,128)(2,1)S(1)} %fusion.31), channel_id=1, replica_groups=mesh['aa'=4,'ba'=8] {'ba'}, dimensions={0}, use_global_device_ids=true | all-gather | bytes 294912 | tf_op jit(solution)/shard_map/all_gather | solution.py:134
  92.9 4.3 %fusion.25 = bf16[1024,768]{0,1:T(8,128)(2,1)S(1)} fusion(bf16[2048,256]{1,0:T(8,128)(2,1)S(1)} %copy-done.16, bf16[2048,256]{1,0:T(8,128)(2,1)S(1)} %copy-done.17, bf16[2048,256]{1,0:T(8,128)(2,1)S(1)} %copy-done.18, f32[1024,2048]{1,0:T(8,128)S(1)} %get-tuple-element.255, f32[2048]{0:T(1024)S(1)} %copy-done.19, f32[1024]{0:T(1024)S(1)} %add_rsqrt_fusion, ...), kind=kOutput, calls=%fused_computation.33 | convolution fusion | flops 3241934848 | bytes 13131776 | tf_op jit(solution)/shard_map/dot_general | solution.py:132
  99.4 43.0 %all-gather.3.cloned.1.call-done = bf16[4096,256]{0,1:T(8,128)(2,1)} async-done(((bf16[1024,256]{0,1:T(8,128)(2,1)}), bf16[4096,256]{0,1:T(8,128)(2,1)}) %all-gather.3.cloned.1.call-update) | async-done | bytes 2097168 | tf_op jit(solution)/shard_map/all_gather | solution.py:75
  142.4 46.1 %all-gather.5.cloned.1.call-done = bf16[4096,256]{0,1:T(8,128)(2,1)} async-done(((bf16[1024,256]{0,1:T(8,128)(2,1)}), bf16[4096,256]{0,1:T(8,128)(2,1)}) %all-gather.5.cloned.1.call-update) | async-done | bytes 2097168 | tf_op jit(solution)/shard_map/all_gather | solution.py:76
  188.4 101.7 %while.18 = (s32[]{:T(128)}, f32[4,1024]{1,0:T(4,128)S(1)}, f32[4,1024]{1,0:T(4,128)S(1)}, f32[1024,4,64]{0,2,1:T(8,128)S(1)}, bf16[4096,256]{0,1:T(8,128)(2,1)}...) while((s32[]{:T(128)}, f32[4,1024]{1,0:T(4,128)S(1)}, ...), condition=%wide.region_5.6_spmd.clone, body=%wide.region_2.5_spmd.clone.sunk | while | flops 1108107264 | bytes 56361128 | solution.py:104
  189.7 8.1 %bitcast_reduce_fusion.2 = (f32[4,1024]{1,0:T(4,128)S(1)}, f32[4,1024,1024]{2,1,0:T(8,128)}) fusion(bf16[1024,4,64]{0,2,1:T(8,128)(2,1)S(1)} %bitcast.131, bf16[1024,4,64]{0,2,1:T(8,128)(2,1)S(1)} %get-tuple-element.340), kind=kOutput, calls=%fused_computation.1.clone.1 | convolution fusion | flops 545255424 | bytes 17842176 | tf_op jit(solution)/shard_map/while/body/eval_jaxpr/qhd,khd->hqk/dot_general | solution.py:89
  197.9 7.4 %fusion.168 = f32[1024,4,64]{0,2,1:T(8,128)S(1)} fusion(bf16[1024,4,64]{0,2,1:T(8,128)(2,1)S(1)} %bitcast.132, f32[4,1024,1024]{2,1,0:T(8,128)} %get-tuple-element.310, f32[4,1024]{1,0:T(4,128)S(1)} %get-tuple-element.336, f32[1024,4,64]{0,2,1:T(8,128)S(1)} %get-tuple-element.327, f32[1024,4]{0,1:T(4,128)S(1)} %get-tuple-element.312, pred[]{:T(512)S(6)} %compare.43), kind=kOutput, calls=%fused_computation.7.clone.1 | convolution fusion | flops 550240256 | bytes 19431424 | tf_op jit(solution)/shard_map/while/body/eval_jaxpr/hqk,khd->qhd/dot_general | solution.py:96
  205.2 8.5 %fusion.166 = f32[4,1024]{1,0:T(4,128)S(1)} fusion(f32[4,1024,1024]{2,1,0:T(8,128)} %get-tuple-element.310, f32[4,1024]{1,0:T(4,128)S(1)} %get-tuple-element.336), kind=kLoop, calls=%fused_computation.4.clone.1 | loop fusion | flops 12578816 | bytes 16809984 | tf_op jit(solution)/shard_map/while/body/eval_jaxpr/reduce_sum | solution.py:95
  215.1 8.1 %bitcast_reduce_fusion.2 = (f32[4,1024]{1,0:T(4,128)S(1)}, f32[4,1024,1024]{2,1,0:T(8,128)}) fusion(bf16[1024,4,64]{0,2,1:T(8,128)(2,1)S(1)} %bitcast.131, bf16[1024,4,64]{0,2,1:T(8,128)(2,1)S(1)} %get-tuple-element.340), kind=kOutput, calls=%fused_computation.1.clone.1 | convolution fusion | flops 545255424 | bytes 17842176 | tf_op jit(solution)/shard_map/while/body/eval_jaxpr/qhd,khd->hqk/dot_general | solution.py:89
  223.3 7.4 %fusion.168 = f32[1024,4,64]{0,2,1:T(8,128)S(1)} fusion(bf16[1024,4,64]{0,2,1:T(8,128)(2,1)S(1)} %bitcast.132, f32[4,1024,1024]{2,1,0:T(8,128)} %get-tuple-element.310, f32[4,1024]{1,0:T(4,128)S(1)} %get-tuple-element.336, f32[1024,4,64]{0,2,1:T(8,128)S(1)} %get-tuple-element.327, f32[1024,4]{0,1:T(4,128)S(1)} %get-tuple-element.312, pred[]{:T(512)S(6)} %compare.43), kind=kOutput, calls=%fused_computation.7.clone.1 | convolution fusion | flops 550240256 | bytes 19431424 | tf_op jit(solution)/shard_map/while/body/eval_jaxpr/hqk,khd->qhd/dot_general | solution.py:96
  230.7 8.5 %fusion.166 = f32[4,1024]{1,0:T(4,128)S(1)} fusion(f32[4,1024,1024]{2,1,0:T(8,128)} %get-tuple-element.310, f32[4,1024]{1,0:T(4,128)S(1)} %get-tuple-element.336), kind=kLoop, calls=%fused_computation.4.clone.1 | loop fusion | flops 12578816 | bytes 16809984 | tf_op jit(solution)/shard_map/while/body/eval_jaxpr/reduce_sum | solution.py:95
  240.5 8.1 %bitcast_reduce_fusion.2 = (f32[4,1024]{1,0:T(4,128)S(1)}, f32[4,1024,1024]{2,1,0:T(8,128)}) fusion(bf16[1024,4,64]{0,2,1:T(8,128)(2,1)S(1)} %bitcast.131, bf16[1024,4,64]{0,2,1:T(8,128)(2,1)S(1)} %get-tuple-element.340), kind=kOutput, calls=%fused_computation.1.clone.1 | convolution fusion | flops 545255424 | bytes 17842176 | tf_op jit(solution)/shard_map/while/body/eval_jaxpr/qhd,khd->hqk/dot_general | solution.py:89
  248.7 7.4 %fusion.168 = f32[1024,4,64]{0,2,1:T(8,128)S(1)} fusion(bf16[1024,4,64]{0,2,1:T(8,128)(2,1)S(1)} %bitcast.132, f32[4,1024,1024]{2,1,0:T(8,128)} %get-tuple-element.310, f32[4,1024]{1,0:T(4,128)S(1)} %get-tuple-element.336, f32[1024,4,64]{0,2,1:T(8,128)S(1)} %get-tuple-element.327, f32[1024,4]{0,1:T(4,128)S(1)} %get-tuple-element.312, pred[]{:T(512)S(6)} %compare.43), kind=kOutput, calls=%fused_computation.7.clone.1 | convolution fusion | flops 550240256 | bytes 19431424 | tf_op jit(solution)/shard_map/while/body/eval_jaxpr/hqk,khd->qhd/dot_general | solution.py:96
  256.1 8.5 %fusion.166 = f32[4,1024]{1,0:T(4,128)S(1)} fusion(f32[4,1024,1024]{2,1,0:T(8,128)} %get-tuple-element.310, f32[4,1024]{1,0:T(4,128)S(1)} %get-tuple-element.336), kind=kLoop, calls=%fused_computation.4.clone.1 | loop fusion | flops 12578816 | bytes 16809984 | tf_op jit(solution)/shard_map/while/body/eval_jaxpr/reduce_sum | solution.py:95
  266.0 8.1 %bitcast_reduce_fusion.2 = (f32[4,1024]{1,0:T(4,128)S(1)}, f32[4,1024,1024]{2,1,0:T(8,128)}) fusion(bf16[1024,4,64]{0,2,1:T(8,128)(2,1)S(1)} %bitcast.131, bf16[1024,4,64]{0,2,1:T(8,128)(2,1)S(1)} %get-tuple-element.340), kind=kOutput, calls=%fused_computation.1.clone.1 | convolution fusion | flops 545255424 | bytes 17842176 | tf_op jit(solution)/shard_map/while/body/eval_jaxpr/qhd,khd->hqk/dot_general | solution.py:89
  274.1 7.4 %fusion.168 = f32[1024,4,64]{0,2,1:T(8,128)S(1)} fusion(bf16[1024,4,64]{0,2,1:T(8,128)(2,1)S(1)} %bitcast.132, f32[4,1024,1024]{2,1,0:T(8,128)} %get-tuple-element.310, f32[4,1024]{1,0:T(4,128)S(1)} %get-tuple-element.336, f32[1024,4,64]{0,2,1:T(8,128)S(1)} %get-tuple-element.327, f32[1024,4]{0,1:T(4,128)S(1)} %get-tuple-element.312, pred[]{:T(512)S(6)} %compare.43), kind=kOutput, calls=%fused_computation.7.clone.1 | convolution fusion | flops 550240256 | bytes 19431424 | tf_op jit(solution)/shard_map/while/body/eval_jaxpr/hqk,khd->qhd/dot_general | solution.py:96
  281.5 8.5 %fusion.166 = f32[4,1024]{1,0:T(4,128)S(1)} fusion(f32[4,1024,1024]{2,1,0:T(8,128)} %get-tuple-element.310, f32[4,1024]{1,0:T(4,128)S(1)} %get-tuple-element.336), kind=kLoop, calls=%fused_computation.4.clone.1 | loop fusion | flops 12578816 | bytes 16809984 | tf_op jit(solution)/shard_map/while/body/eval_jaxpr/reduce_sum | solution.py:95
  292.0 32.6 %reduce-scatter.2.cloned.1.call-done = bf16[128,128]{1,0:T(8,128)(2,1)} async-done(((bf16[1024,128]{1,0:T(8,128)(2,1)}), bf16[128,128]{1,0:T(8,128)(2,1)}) %reduce-scatter.2.cloned.1.call-update) | async-done | bytes 32784 | tf_op jit(solution)/shard_map/reduce_scatter | solution.py:140
  (124 shorter events, 40.4 us)
Async XLA Ops:
  6.5 83.1 %copy-start = (bf16[128,2048]{1,0:T(8,128)(2,1)S(1)}, bf16[128,2048]{1,0:T(8,128)(2,1)}, u32[]{:S(2)}) copy-start(bf16[128,2048]{1,0:T(8,128)(2,1)} %param.23) | copy-start | bytes 1572868
  6.5 135.8 %all-gather.3.cloned.1.call-start = ((), (), s32[]{:S(2)}) async-start(), calls=%async_computation.1 | async-start | bytes 2621440 | tf_op jit(solution)/shard_map/all_gather | solution.py:75
  6.5 10.9 %collective-permute-start = (bf16[1,4,128,256]{3,2,1,0:T(8,128)(2,1)}, bf16[1,4,128,256]{3,2,1,0:T(8,128)(2,1)S(1)}, u32[]{:S(2)}, u32[]{:S(2)}) collective-permute-start(bf16[1,4,128,256]{3,2,1,0:T(8,128)(2,1)} %param.16), channel_id=1, source_target_pairs={{0,8},{8,16},{16,24},{1,9},{9,17},{17,25},{2,10},{10,18},{18,26},{... | collective-permute-start | bytes 786440 | tf_op jit(solution)/shard_map/ppermute | solution.py:18
  11.6 9.9 %collective-permute-start.1 = (bf16[1,4,128,256]{3,2,1,0:T(8,128)(2,1)}, bf16[1,4,128,256]{3,2,1,0:T(8,128)(2,1)S(1)}, u32[]{:S(2)}, u32[]{:S(2)}) collective-permute-start(bf16[1,4,128,256]{3,2,1,0:T(8,128)(2,1)} %param.16), channel_id=1, source_target_pairs={{8,0},{16,8},{24,16},{9,1},{17,9},{25,17},{10,2},{18,10},{26,18},{... | collective-permute-start | bytes 786440 | tf_op jit(solution)/shard_map/ppermute | solution.py:20
  21.6 4.8 %collective-permute-start.2 = (bf16[3,1,128,256]{3,2,1,0:T(8,128)(2,1)S(1)}, bf16[3,1,128,256]{3,2,1,0:T(8,128)(2,1)S(1)}, u32[]{:S(2)}, u32[]{:S(2)}) collective-permute-start(bf16[3,1,128,256]{3,2,1,0:T(8,128)(2,1)S(1)} %get-tuple-element.248), channel_id=1, source_target_pairs={{0,1},{1,2},{2,3},{3,4},{4,5},{5,6},{6,7},{8,9},{9,10},{10,11},{11... | collective-permute-start | bytes 589832 | tf_op jit(solution)/shard_map/ppermute | solution.py:18
  22.9 5.1 %collective-permute-start.3 = (bf16[3,1,128,256]{3,2,1,0:T(8,128)(2,1)S(1)}, bf16[3,1,128,256]{3,2,1,0:T(8,128)(2,1)S(1)}, u32[]{:S(2)}, u32[]{:S(2)}) collective-permute-start(bf16[3,1,128,256]{3,2,1,0:T(8,128)(2,1)S(1)} %get-tuple-element.247), channel_id=1, source_target_pairs={{1,0},{2,1},{3,2},{4,3},{5,4},{6,5},{7,6},{9,8},{10,9},{11,10},{12... | collective-permute-start | bytes 589832 | tf_op jit(solution)/shard_map/ppermute | solution.py:20
  28.5 1.0 copy-start.10
  33.6 22.5 %copy-start.2 = (bf16[3,3,3,256,256]{4,3,2,1,0:T(8,128)(2,1)S(1)}, bf16[3,3,3,256,256]{4,3,2,1,0:T(8,128)(2,1)}, u32[]{:S(2)}) copy-start(bf16[3,3,3,256,256]{4,3,2,1,0:T(8,128)(2,1)} %param.19) | copy-start | bytes 10616836
  36.8 7.3 %collective-permute-start.4 = (bf16[1,4,128,256]{3,2,1,0:T(8,128)(2,1)S(1)}, bf16[1,4,128,256]{3,2,1,0:T(8,128)(2,1)S(1)}, u32[]{:S(2)}, u32[]{:S(2)}) collective-permute-start(bf16[1,4,128,256]{3,2,1,0:T(8,128)(2,1)S(1)} %fusion.66), channel_id=1, source_target_pairs={{0,8},{8,16},{16,24},{1,9},{9,17},{17,25},{2,10},{10,18},{18,26},{... | collective-permute-start | bytes 786440 | tf_op jit(solution)/shard_map/ppermute | solution.py:18
  40.3 8.3 %collective-permute-start.5 = (bf16[1,4,128,256]{3,2,1,0:T(8,128)(2,1)S(1)}, bf16[1,4,128,256]{3,2,1,0:T(8,128)(2,1)S(1)}, u32[]{:S(2)}, u32[]{:S(2)}) collective-permute-start(bf16[1,4,128,256]{3,2,1,0:T(8,128)(2,1)S(1)} %fusion.66), channel_id=1, source_target_pairs={{8,0},{16,8},{24,16},{9,1},{17,9},{25,17},{10,2},{18,10},{26,18},{... | collective-permute-start | bytes 786440 | tf_op jit(solution)/shard_map/ppermute | solution.py:20
  49.3 9.1 %collective-permute-start.6 = (bf16[3,1,128,256]{3,2,1,0:T(8,128)(2,1)}, bf16[3,1,128,256]{3,2,1,0:T(8,128)(2,1)}, u32[]{:S(2)}, u32[]{:S(2)}) collective-permute-start(bf16[3,1,128,256]{3,2,1,0:T(8,128)(2,1)} %get-tuple-element.246), channel_id=1, source_target_pairs={{0,1},{1,2},{2,3},{3,4},{4,5},{5,6},{6,7},{8,9},{9,10},{10,11},{11... | collective-permute-start | bytes 589832 | tf_op jit(solution)/shard_map/ppermute | solution.py:18
  54.6 5.0 %collective-permute-start.7 = (bf16[3,1,128,256]{3,2,1,0:T(8,128)(2,1)}, bf16[3,1,128,256]{3,2,1,0:T(8,128)(2,1)S(1)}, u32[]{:S(2)}, u32[]{:S(2)}) collective-permute-start(bf16[3,1,128,256]{3,2,1,0:T(8,128)(2,1)} %get-tuple-element.245), channel_id=1, source_target_pairs={{1,0},{2,1},{3,2},{4,3},{5,4},{6,5},{7,6},{9,8},{10,9},{11,10},{12... | collective-permute-start | bytes 589832 | tf_op jit(solution)/shard_map/ppermute | solution.py:20
  62.0 1.1 copy-start.9
  63.1 1.0 copy-start.8
  64.5 1.0 copy-start.7
  64.8 1.1 copy-start.6
  65.9 1.0 copy-start.11
  65.9 1.1 copy-start.21
  66.3 1.1 copy-start.5
  67.3 1.0 copy-start.4
  68.3 1.0 copy-start.3
  68.7 1.0 copy-start.14
  70.8 2.7 copy-start.15
  70.8 18.9 %copy-start.12 = (f32[2048]{0:T(1024)S(1)}, f32[2048]{0:T(1024)}, u32[]{:S(2)}) copy-start(f32[2048]{0:T(1024)} %param.24) | copy-start | bytes 24580
  91.0 1.3 copy-start.16
  91.0 1.5 copy-start.17
  91.0 1.8 copy-start.18
  91.0 1.8 copy-start.19
  98.3 90.1 %all-gather.5.cloned.1.call-start = ((), (), s32[]{:S(2)}) async-start(), calls=%async_computation.2 | async-start | bytes 2621440 | tf_op jit(solution)/shard_map/all_gather | solution.py:76
  99.1 225.6 %reduce-scatter.2.cloned.1.call-start = ((), (), s32[]{:S(2)}) async-start(), calls=%async_computation.3 | async-start | bytes 294912 | tf_op jit(solution)/shard_map/reduce_scatter | solution.py:140
  290.1 0.8 copy-start.13
  290.1 35.9 %copy-start.1 = (bf16[128,2048]{1,0:T(8,128)(2,1)S(1)}, bf16[128,2048]{1,0:T(8,128)(2,1)}, u32[]{:S(2)}) copy-start(bf16[128,2048]{1,0:T(8,128)(2,1)} %param.23) | copy-start | bytes 1572868
  (1 other events, 0.7 us)
Sparse Core Ops, SparseCore 0:
  98.4 43.8 all-gather.2
  143.9 44.4 all-gather.4
  292.1 32.4 reduce-scatter.1
where the time goes:
time: 334 us; the launch traced here: 333 us
  waiting for transfers between devices  140 us (42%)
  matrix products  78.4 us (23%)
  other arithmetic  45.5 us (14%)
  starting transfers between devices  20.9 us (6%)
  local copies, waits for them, and re-layouts  19.1 us (6%)
  blocking collectives  15 us (4%)
  between operations  13.7 us (4%)
    all_gather x1, waiting for transfers between devices, attend(): value_rows = lax.all_gather(values, 'aa', axis=0, tiled=True)  46.1 us
    all_gather x1, waiting for transfers between devices, attend(): key_rows = lax.all_gather(keys, 'aa', axis=0, tiled=True)  43 us
    reduce_sum x4, other arithmetic, one_step(): denom = denom * fade + probs.sum(-1)  34.1 us
    reduce_scatter x1, waiting for transfers between devices, on_device(): lax.psum_scatter(jnp.dot(attended, w_velocity, preferred_element_type=jnp...  32.6 us
    dot_general x4, matrix products, one_step(): jnp.einsum('qhd,khd->hqk', query_heads, key_block, preferred_element_type...  32.6 us
    dot_general x4, matrix products, one_step(): jnp.einsum('hqk,khd->qhd', probs.astype(jnp.bfloat16), value_block, prefe...  29.5 us
    ppermute x4, starting transfers between devices, with_halo(): lax.ppermute(tail, axis, [(i, (i + 1) % count) for i in range(ends)])  15.2 us
    all_gather x1, blocking collectives, on_device(): lax.all_gather(latents, 'ba', axis=0, tiled=True)  15 us
  transfers between devices with their start and end apart: 11, of which 9 were waited for; matrix products, arithmetic and copies ran while one was open for 2% of the time, Pallas kernels for 0%

commit v1 on v0

--- a/solution.py
+++ b/solution.py
@@ -5,6 +5,12 @@
 from jax.sharding import PartitionSpec as P
 
 HEAD_DIM = 64
+
+
+def tiled_gather(x, axis, dim):
+    size = lax.axis_size(axis)
+    repeats = [size if d == dim else 1 for d in range(x.ndim)]
+    return lax.all_to_all(jnp.tile(x, repeats), axis, split_axis=dim, concat_axis=dim, tiled=True)
 
 
 def with_halo(cells, sides, width):
@@ -73,7 +79,7 @@
         jnp.zeros((rows, heads, HEAD_DIM), jnp.float32),
     )
     key_rows = lax.all_gather(keys, "aa", axis=0, tiled=True)
-    value_rows = lax.all_gather(values, "aa", axis=0, tiled=True)
+    value_rows = tiled_gather(values, "aa", 0)
     count = key_rows.shape[0]
     block = math.gcd(count, 1024)
 

time: 334 us -> 339 us (1.015)
  local copies, waits for them, and re-layouts: 19.1 us -> 28.9 us
  waiting for transfers between devices: 140 us -> 131 us
  starting transfers between devices: 20.9 us -> 25.3 us
    all_to_all x0 -> x1, waiting for transfers between devices: none -> 81.7 us  [tiled_gather(): lax.all_to_all(jnp.tile(x, repeats), axis, split_axis=dim, concat_axis=di...]
    all_gather x1 -> x0, waiting for transfers between devices: 46.1 us -> none  [attend(): value_rows = lax.all_gather(values, 'aa', axis=0, tiled=True)]
    all_gather x1, waiting for transfers between devices: 43 us -> 0.01 us  [attend(): key_rows = lax.all_gather(keys, 'aa', axis=0, tiled=True)]
    all_to_all x0 -> x1, starting transfers between devices: none -> 4.43 us  [tiled_gather(): lax.all_to_all(jnp.tile(x, repeats), axis, split_axis=dim, concat_axis=di...]
    dynamic_slice x0 -> x4, local copies, waits for them, and re-layouts: none -> 4.32 us  [one_step(): lax.dynamic_slice_in_dim(key_rows, index * block, block, 0)]
    all_to_all x0 -> x1, local copies, waits for them, and re-layouts: none -> 3.95 us  [tiled_gather(): lax.all_to_all(jnp.tile(x, repeats), axis, split_axis=dim, concat_axis=di...]
  transfers between devices with their start and end apart: 11 -> 11, of which waited for: 9 -> 8; matrix products, arithmetic and copies ran while one was open for 2% -> 3% of each run, Pallas kernels for 0% -> 0%
where the time goes in v1:
time: 339 us; the launch traced here: 337 us
  waiting for transfers between devices  131 us (39%)
  matrix products  77.5 us (23%)
  other arithmetic  45.4 us (13%)
  local copies, waits for them, and re-layouts  28.9 us (9%)
  starting transfers between devices  25.3 us (7%)
  blocking collectives  15 us (4%)
  between operations  14.1 us (4%)
    all_to_all x1, waiting for transfers between devices, tiled_gather(): lax.all_to_all(jnp.tile(x, repeats), axis, split_axis=dim, concat_axis=di...  81.7 us
    reduce_sum x4, other arithmetic, one_step(): denom = denom * fade + probs.sum(-1)  34 us
    dot_general x4, matrix products, one_step(): jnp.einsum('qhd,khd->hqk', query_heads, key_block, preferred_element_type...  32.6 us
    reduce_scatter x1, waiting for transfers between devices, on_device(): lax.psum_scatter(jnp.dot(attended, w_velocity, preferred_element_type=jnp...  31.1 us
    dot_general x4, matrix products, one_step(): jnp.einsum('hqk,khd->qhd', probs.astype(jnp.bfloat16), value_block, prefe...  29.5 us
    ppermute x4, starting transfers between devices, with_halo(): lax.ppermute(tail, axis, [(i, (i + 1) % count) for i in range(ends)])  15.2 us
    all_gather x1, blocking collectives, on_device(): lax.all_gather(latents, 'ba', axis=0, tiled=True)  15 us
    ppermute x4, waiting for transfers between devices, with_halo(): lax.ppermute(head, axis, [((i + 1) % count, i) for i in range(ends)])  10.3 us
  transfers between devices with their start and end apart: 11, of which 8 were waited for; matrix products, arithmetic and copies ran while one was open for 3% of the time, Pallas kernels for 0%

profile of v1, /device:TPU:0, one launch (start us, length us, event | category | flops | bytes accessed | tf_op | source)
XLA Modules:
  0.0 337.2 jit_solution(13064511340146854821)
XLA Ops:
  6.5 5.1 %collective-permute-start = (bf16[1,4,128,256]{3,2,1,0:T(8,128)(2,1)}, bf16[1,4,128,256]{3,2,1,0:T(8,128)(2,1)S(1)}, u32[]{:S(2)}, u32[]{:S(2)}) collective-permute-start(bf16[1,4,128,256]{3,2,1,0:T(8,128)(2,1)} %param.16), channel_id=1, source_target_pairs={{0,8},{8,16},{16,24},{1,9},{9,17},{17,25},{2,10},{10,18},{18,26},{... | collective-permute-start | bytes 786440 | tf_op jit(solution)/shard_map/ppermute | solution.py:24
  12.9 4.5 %collective-permute-done = bf16[1,4,128,256]{3,2,1,0:T(8,128)(2,1)S(1)} collective-permute-done((bf16[1,4,128,256]{3,2,1,0:T(8,128)(2,1)}, bf16[1,4,128,256]{3,2,1,0:T(8,128)(2,1)S(1)}, u32[]{:S(2)}, u32[]{:S(2)}) %collective-permute-start) | collective-permute-done | bytes 262176 | tf_op jit(solution)/shard_map/ppermute | solution.py:24
  18.5 3.0 collective-permute-done.1
  24.2 2.2 fusion.102
  26.4 1.6 collective-permute-done.3
  33.6 2.1 fusion.69
  36.8 3.5 %collective-permute-start.4 = (bf16[1,4,128,256]{3,2,1,0:T(8,128)(2,1)S(1)}, bf16[1,4,128,256]{3,2,1,0:T(8,128)(2,1)S(1)}, u32[]{:S(2)}, u32[]{:S(2)}) collective-permute-start(bf16[1,4,128,256]{3,2,1,0:T(8,128)(2,1)S(1)} %fusion.66), channel_id=1, source_target_pairs={{0,8},{8,16},{16,24},{1,9},{9,17},{17,25},{2,10},{10,18},{18,26},{... | collective-permute-start | bytes 786440 | tf_op jit(solution)/shard_map/ppermute | solution.py:24
  41.6 2.6 collective-permute-done.4
  44.2 4.4 %collective-permute-done.5 = bf16[1,4,128,256]{3,2,1,0:T(8,128)(2,1)S(1)} collective-permute-done((bf16[1,4,128,256]{3,2,1,0:T(8,128)(2,1)S(1)}, bf16[1,4,128,256]{3,2,1,0:T(8,128)(2,1)S(1)}, u32[]{:S(2)}, u32[]{:S(2)}) %collective-permute-start.5) | collective-permute-done | bytes 262176 | tf_op jit(solution)/shard_map/ppermute | solution.py:26
  49.3 5.3 %collective-permute-start.6 = (bf16[3,1,128,256]{3,2,1,0:T(8,128)(2,1)}, bf16[3,1,128,256]{3,2,1,0:T(8,128)(2,1)}, u32[]{:S(2)}, u32[]{:S(2)}) collective-permute-start(bf16[3,1,128,256]{3,2,1,0:T(8,128)(2,1)} %get-tuple-element.265), channel_id=1, source_target_pairs={{0,1},{1,2},{2,3},{3,4},{4,5},{5,6},{6,7},{8,9},{9,10},{10,11},{11... | collective-permute-start | bytes 589832 | tf_op jit(solution)/shard_map/ppermute | solution.py:24
  56.1 1.7 fusion.101
  70.9 2.2 fusion.98
  73.8 15.0 %all_gather.6 = bf16[1024,128]{1,0:T(8,128)(2,1)S(1)} all-gather(bf16[128,128]{1,0:T(8,128)(2,1)S(1)} %fusion.31), channel_id=1, replica_groups=mesh['aa'=4,'ba'=8] {'ba'}, dimensions={0}, use_global_device_ids=true | all-gather | bytes 294912 | tf_op jit(solution)/shard_map/all_gather | solution.py:140
  92.0 4.3 %fusion.25 = bf16[1024,768]{0,1:T(8,128)(2,1)S(1)} fusion(bf16[2048,256]{1,0:T(8,128)(2,1)S(1)} %copy-done.17, bf16[2048,256]{1,0:T(8,128)(2,1)S(1)} %copy-done.18, bf16[2048,256]{1,0:T(8,128)(2,1)S(1)} %copy-done.19, f32[1024,2048]{1,0:T(8,128)S(1)} %get-tuple-element.274, f32[2048]{0:T(1024)S(1)} %copy-done.20, f32[1024]{0:T(1024)S(1)} %add_rsqrt_fusion, ...), kind=kOutput, calls=%fused_computation.33 | convolution fusion | flops 3241934848 | bytes 13131776 | tf_op jit(solution)/shard_map/dot_general | solution.py:138
  97.2 1.6 tile.2
  98.8 4.4 %all-to-all-start = ((bf16[4,1024,256]{1,2,0:T(8,128)(2,1)}), bf16[4,1024,256]{1,2,0:T(8,128)(2,1)}, u32[]{:S(2)}, u32[]{:S(2)}) async-start(bf16[4,1024,256]{1,2,0:T(8,128)(2,1)} %tile.2), calls=%async_computation | async-start | bytes 4194304 | tf_op jit(solution)/shard_map/all_to_all | solution.py:13
  104.3 81.7 %all-to-all-done = bf16[4,1024,256]{1,2,0:T(8,128)(2,1)} async-done(((bf16[4,1024,256]{1,2,0:T(8,128)(2,1)}), bf16[4,1024,256]{1,2,0:T(8,128)(2,1)}, u32[]{:S(2)}, u32[]{:S(2)}) %all-to-all-start) | async-done | bytes 2097184 | tf_op jit(solution)/shard_map/all_to_all | solution.py:13
  186.0 3.9 %copy.75 = bf16[4,1024,256]{2,1,0:T(8,128)(2,1)} copy(bf16[4,1024,256]{1,2,0:T(8,128)(2,1)} %all-to-all-done) | data formatting | bytes 4194304 | tf_op jit(solution)/shard_map/all_to_all | solution.py:13
  190.0 106.0 %while.18 = (s32[]{:T(128)}, f32[4,1024]{1,0:T(4,128)S(1)}, f32[4,1024]{1,0:T(4,128)S(1)}, f32[1024,4,64]{0,2,1:T(8,128)S(1)}, bf16[4096,256]{0,1:T(8,128)(2,1)}...) while((s32[]{:T(128)}, f32[4,1024]{1,0:T(4,128)S(1)}, ...), condition=%wide.region_5.6_spmd.clone, body=%wide.region_2.5_spmd.clone.sunk | while | flops 1108107264 | bytes 57409708 | solution.py:110
  191.1 8.1 %bitcast_reduce_fusion.2 = (f32[4,1024]{1,0:T(4,128)S(1)}, f32[4,1024,1024]{2,1,0:T(8,128)}) fusion(bf16[1024,4,64]{0,2,1:T(8,128)(2,1)S(1)} %bitcast.132, bf16[1024,4,64]{0,2,1:T(8,128)(2,1)S(1)} %get-tuple-element.355), kind=kOutput, calls=%fused_computation.1.clone.1 | convolution fusion | flops 545255424 | bytes 17842176 | tf_op jit(solution)/shard_map/while/body/eval_jaxpr/qhd,khd->hqk/dot_general | solution.py:95
  200.5 7.4 %fusion.168 = f32[1024,4,64]{0,2,1:T(8,128)S(1)} fusion(bf16[1024,4,64]{0,2,1:T(8,128)(2,1)S(1)} %bitcast.133, f32[4,1024,1024]{2,1,0:T(8,128)} %get-tuple-element.326, f32[4,1024]{1,0:T(4,128)S(1)} %get-tuple-element.351, f32[1024,4,64]{0,2,1:T(8,128)S(1)} %get-tuple-element.342, f32[1024,4]{0,1:T(4,128)S(1)} %get-tuple-element.327, pred[]{:T(512)S(6)} %compare.43), kind=kOutput, calls=%fused_computation.7.clone.1 | convolution fusion | flops 550240256 | bytes 19431424 | tf_op jit(solution)/shard_map/while/body/eval_jaxpr/hqk,khd->qhd/dot_general | solution.py:102
  207.9 8.5 %fusion.166 = f32[4,1024]{1,0:T(4,128)S(1)} fusion(f32[4,1024,1024]{2,1,0:T(8,128)} %get-tuple-element.326, f32[4,1024]{1,0:T(4,128)S(1)} %get-tuple-element.351), kind=kLoop, calls=%fused_computation.4.clone.1 | loop fusion | flops 12578816 | bytes 16809984 | tf_op jit(solution)/shard_map/while/body/eval_jaxpr/reduce_sum | solution.py:101
  217.6 8.1 %bitcast_reduce_fusion.2 = (f32[4,1024]{1,0:T(4,128)S(1)}, f32[4,1024,1024]{2,1,0:T(8,128)}) fusion(bf16[1024,4,64]{0,2,1:T(8,128)(2,1)S(1)} %bitcast.132, bf16[1024,4,64]{0,2,1:T(8,128)(2,1)S(1)} %get-tuple-element.355), kind=kOutput, calls=%fused_computation.1.clone.1 | convolution fusion | flops 545255424 | bytes 17842176 | tf_op jit(solution)/shard_map/while/body/eval_jaxpr/qhd,khd->hqk/dot_general | solution.py:95
  227.0 7.4 %fusion.168 = f32[1024,4,64]{0,2,1:T(8,128)S(1)} fusion(bf16[1024,4,64]{0,2,1:T(8,128)(2,1)S(1)} %bitcast.133, f32[4,1024,1024]{2,1,0:T(8,128)} %get-tuple-element.326, f32[4,1024]{1,0:T(4,128)S(1)} %get-tuple-element.351, f32[1024,4,64]{0,2,1:T(8,128)S(1)} %get-tuple-element.342, f32[1024,4]{0,1:T(4,128)S(1)} %get-tuple-element.327, pred[]{:T(512)S(6)} %compare.43), kind=kOutput, calls=%fused_computation.7.clone.1 | convolution fusion | flops 550240256 | bytes 19431424 | tf_op jit(solution)/shard_map/while/body/eval_jaxpr/hqk,khd->qhd/dot_general | solution.py:102
  234.4 8.5 %fusion.166 = f32[4,1024]{1,0:T(4,128)S(1)} fusion(f32[4,1024,1024]{2,1,0:T(8,128)} %get-tuple-element.326, f32[4,1024]{1,0:T(4,128)S(1)} %get-tuple-element.351), kind=kLoop, calls=%fused_computation.4.clone.1 | loop fusion | flops 12578816 | bytes 16809984 | tf_op jit(solution)/shard_map/while/body/eval_jaxpr/reduce_sum | solution.py:101
  244.1 8.1 %bitcast_reduce_fusion.2 = (f32[4,1024]{1,0:T(4,128)S(1)}, f32[4,1024,1024]{2,1,0:T(8,128)}) fusion(bf16[1024,4,64]{0,2,1:T(8,128)(2,1)S(1)} %bitcast.132, bf16[1024,4,64]{0,2,1:T(8,128)(2,1)S(1)} %get-tuple-element.355), kind=kOutput, calls=%fused_computation.1.clone.1 | convolution fusion | flops 545255424 | bytes 17842176 | tf_op jit(solution)/shard_map/while/body/eval_jaxpr/qhd,khd->hqk/dot_general | solution.py:95
  253.5 7.4 %fusion.168 = f32[1024,4,64]{0,2,1:T(8,128)S(1)} fusion(bf16[1024,4,64]{0,2,1:T(8,128)(2,1)S(1)} %bitcast.133, f32[4,1024,1024]{2,1,0:T(8,128)} %get-tuple-element.326, f32[4,1024]{1,0:T(4,128)S(1)} %get-tuple-element.351, f32[1024,4,64]{0,2,1:T(8,128)S(1)} %get-tuple-element.342, f32[1024,4]{0,1:T(4,128)S(1)} %get-tuple-element.327, pred[]{:T(512)S(6)} %compare.43), kind=kOutput, calls=%fused_computation.7.clone.1 | convolution fusion | flops 550240256 | bytes 19431424 | tf_op jit(solution)/shard_map/while/body/eval_jaxpr/hqk,khd->qhd/dot_general | solution.py:102
  260.9 8.5 %fusion.166 = f32[4,1024]{1,0:T(4,128)S(1)} fusion(f32[4,1024,1024]{2,1,0:T(8,128)} %get-tuple-element.326, f32[4,1024]{1,0:T(4,128)S(1)} %get-tuple-element.351), kind=kLoop, calls=%fused_computation.4.clone.1 | loop fusion | flops 12578816 | bytes 16809984 | tf_op jit(solution)/shard_map/while/body/eval_jaxpr/reduce_sum | solution.py:101
  270.6 8.1 %bitcast_reduce_fusion.2 = (f32[4,1024]{1,0:T(4,128)S(1)}, f32[4,1024,1024]{2,1,0:T(8,128)}) fusion(bf16[1024,4,64]{0,2,1:T(8,128)(2,1)S(1)} %bitcast.132, bf16[1024,4,64]{0,2,1:T(8,128)(2,1)S(1)} %get-tuple-element.355), kind=kOutput, calls=%fused_computation.1.clone.1 | convolution fusion | flops 545255424 | bytes 17842176 | tf_op jit(solution)/shard_map/while/body/eval_jaxpr/qhd,khd->hqk/dot_general | solution.py:95
  280.0 7.4 %fusion.168 = f32[1024,4,64]{0,2,1:T(8,128)S(1)} fusion(bf16[1024,4,64]{0,2,1:T(8,128)(2,1)S(1)} %bitcast.133, f32[4,1024,1024]{2,1,0:T(8,128)} %get-tuple-element.326, f32[4,1024]{1,0:T(4,128)S(1)} %get-tuple-element.351, f32[1024,4,64]{0,2,1:T(8,128)S(1)} %get-tuple-element.342, f32[1024,4]{0,1:T(4,128)S(1)} %get-tuple-element.327, pred[]{:T(512)S(6)} %compare.43), kind=kOutput, calls=%fused_computation.7.clone.1 | convolution fusion | flops 550240256 | bytes 19431424 | tf_op jit(solution)/shard_map/while/body/eval_jaxpr/hqk,khd->qhd/dot_general | solution.py:102
  287.4 8.5 %fusion.166 = f32[4,1024]{1,0:T(4,128)S(1)} fusion(f32[4,1024,1024]{2,1,0:T(8,128)} %get-tuple-element.326, f32[4,1024]{1,0:T(4,128)S(1)} %get-tuple-element.351), kind=kLoop, calls=%fused_computation.4.clone.1 | loop fusion | flops 12578816 | bytes 16809984 | tf_op jit(solution)/shard_map/while/body/eval_jaxpr/reduce_sum | solution.py:101
  297.9 31.1 %reduce-scatter.2.cloned.1.call-done = bf16[128,128]{1,0:T(8,128)(2,1)} async-done(((bf16[1024,128]{1,0:T(8,128)(2,1)}), bf16[128,128]{1,0:T(8,128)(2,1)}) %reduce-scatter.2.cloned.1.call-update) | async-done | bytes 32784 | tf_op jit(solution)/shard_map/reduce_scatter | solution.py:146
  (135 shorter events, 46.6 us)
Async XLA Ops:
  6.5 82.2 %copy-start = (bf16[128,2048]{1,0:T(8,128)(2,1)S(1)}, bf16[128,2048]{1,0:T(8,128)(2,1)}, u32[]{:S(2)}) copy-start(bf16[128,2048]{1,0:T(8,128)(2,1)} %param.23) | copy-start | bytes 1572868
  6.5 10.9 %collective-permute-start = (bf16[1,4,128,256]{3,2,1,0:T(8,128)(2,1)}, bf16[1,4,128,256]{3,2,1,0:T(8,128)(2,1)S(1)}, u32[]{:S(2)}, u32[]{:S(2)}) collective-permute-start(bf16[1,4,128,256]{3,2,1,0:T(8,128)(2,1)} %param.16), channel_id=1, source_target_pairs={{0,8},{8,16},{16,24},{1,9},{9,17},{17,25},{2,10},{10,18},{18,26},{... | collective-permute-start | bytes 786440 | tf_op jit(solution)/shard_map/ppermute | solution.py:24
  11.6 9.9 %collective-permute-start.1 = (bf16[1,4,128,256]{3,2,1,0:T(8,128)(2,1)}, bf16[1,4,128,256]{3,2,1,0:T(8,128)(2,1)S(1)}, u32[]{:S(2)}, u32[]{:S(2)}) collective-permute-start(bf16[1,4,128,256]{3,2,1,0:T(8,128)(2,1)} %param.16), channel_id=1, source_target_pairs={{8,0},{16,8},{24,16},{9,1},{17,9},{25,17},{10,2},{18,10},{26,18},{... | collective-permute-start | bytes 786440 | tf_op jit(solution)/shard_map/ppermute | solution.py:26
  21.6 4.8 %collective-permute-start.2 = (bf16[3,1,128,256]{3,2,1,0:T(8,128)(2,1)S(1)}, bf16[3,1,128,256]{3,2,1,0:T(8,128)(2,1)S(1)}, u32[]{:S(2)}, u32[]{:S(2)}) collective-permute-start(bf16[3,1,128,256]{3,2,1,0:T(8,128)(2,1)S(1)} %get-tuple-element.267), channel_id=1, source_target_pairs={{0,1},{1,2},{2,3},{3,4},{4,5},{5,6},{6,7},{8,9},{9,10},{10,11},{11... | collective-permute-start | bytes 589832 | tf_op jit(solution)/shard_map/ppermute | solution.py:24
  22.9 5.1 %collective-permute-start.3 = (bf16[3,1,128,256]{3,2,1,0:T(8,128)(2,1)S(1)}, bf16[3,1,128,256]{3,2,1,0:T(8,128)(2,1)S(1)}, u32[]{:S(2)}, u32[]{:S(2)}) collective-permute-start(bf16[3,1,128,256]{3,2,1,0:T(8,128)(2,1)S(1)} %get-tuple-element.266), channel_id=1, source_target_pairs={{1,0},{2,1},{3,2},{4,3},{5,4},{6,5},{7,6},{9,8},{10,9},{11,10},{12... | collective-permute-start | bytes 589832 | tf_op jit(solution)/shard_map/ppermute | solution.py:26
  28.5 1.0 copy-start.10
  33.6 22.5 %copy-start.2 = (bf16[3,3,3,256,256]{4,3,2,1,0:T(8,128)(2,1)S(1)}, bf16[3,3,3,256,256]{4,3,2,1,0:T(8,128)(2,1)}, u32[]{:S(2)}) copy-start(bf16[3,3,3,256,256]{4,3,2,1,0:T(8,128)(2,1)} %param.19) | copy-start | bytes 10616836
  36.8 7.3 %collective-permute-start.4 = (bf16[1,4,128,256]{3,2,1,0:T(8,128)(2,1)S(1)}, bf16[1,4,128,256]{3,2,1,0:T(8,128)(2,1)S(1)}, u32[]{:S(2)}, u32[]{:S(2)}) collective-permute-start(bf16[1,4,128,256]{3,2,1,0:T(8,128)(2,1)S(1)} %fusion.66), channel_id=1, source_target_pairs={{0,8},{8,16},{16,24},{1,9},{9,17},{17,25},{2,10},{10,18},{18,26},{... | collective-permute-start | bytes 786440 | tf_op jit(solution)/shard_map/ppermute | solution.py:24
  40.3 8.3 %collective-permute-start.5 = (bf16[1,4,128,256]{3,2,1,0:T(8,128)(2,1)S(1)}, bf16[1,4,128,256]{3,2,1,0:T(8,128)(2,1)S(1)}, u32[]{:S(2)}, u32[]{:S(2)}) collective-permute-start(bf16[1,4,128,256]{3,2,1,0:T(8,128)(2,1)S(1)} %fusion.66), channel_id=1, source_target_pairs={{8,0},{16,8},{24,16},{9,1},{17,9},{25,17},{10,2},{18,10},{26,18},{... | collective-permute-start | bytes 786440 | tf_op jit(solution)/shard_map/ppermute | solution.py:26
  49.3 9.1 %collective-permute-start.6 = (bf16[3,1,128,256]{3,2,1,0:T(8,128)(2,1)}, bf16[3,1,128,256]{3,2,1,0:T(8,128)(2,1)}, u32[]{:S(2)}, u32[]{:S(2)}) collective-permute-start(bf16[3,1,128,256]{3,2,1,0:T(8,128)(2,1)} %get-tuple-element.265), channel_id=1, source_target_pairs={{0,1},{1,2},{2,3},{3,4},{4,5},{5,6},{6,7},{8,9},{9,10},{10,11},{11... | collective-permute-start | bytes 589832 | tf_op jit(solution)/shard_map/ppermute | solution.py:24
  54.6 5.0 %collective-permute-start.7 = (bf16[3,1,128,256]{3,2,1,0:T(8,128)(2,1)}, bf16[3,1,128,256]{3,2,1,0:T(8,128)(2,1)S(1)}, u32[]{:S(2)}, u32[]{:S(2)}) collective-permute-start(bf16[3,1,128,256]{3,2,1,0:T(8,128)(2,1)} %get-tuple-element.264), channel_id=1, source_target_pairs={{1,0},{2,1},{3,2},{4,3},{5,4},{6,5},{7,6},{9,8},{10,9},{11,10},{12... | collective-permute-start | bytes 589832 | tf_op jit(solution)/shard_map/ppermute | solution.py:26
  62.0 1.1 copy-start.9
  63.2 1.0 copy-start.8
  64.6 1.0 copy-start.7
  64.9 1.1 copy-start.6
  66.0 1.0 copy-start.11
  66.0 1.1 copy-start.22
  66.4 1.0 copy-start.5
  67.4 1.0 copy-start.4
  68.4 1.0 copy-start.3
  68.8 1.0 copy-start.15
  70.8 2.7 copy-start.12
  70.8 2.7 copy-start.16
  70.8 17.9 %copy-start.13 = (f32[2048]{0:T(1024)S(1)}, f32[2048]{0:T(1024)}, u32[]{:S(2)}) copy-start(f32[2048]{0:T(1024)} %param.24) | copy-start | bytes 24580
  90.1 1.3 copy-start.17
  90.1 1.5 copy-start.18
  90.1 1.8 copy-start.19
  90.2 1.8 copy-start.20
  98.8 87.2 %all-to-all-start = ((bf16[4,1024,256]{1,2,0:T(8,128)(2,1)}), bf16[4,1024,256]{1,2,0:T(8,128)(2,1)}, u32[]{:S(2)}, u32[]{:S(2)}) async-start(bf16[4,1024,256]{1,2,0:T(8,128)(2,1)} %tile.2), calls=%async_computation | async-start | bytes 4194304 | tf_op jit(solution)/shard_map/all_to_all | solution.py:13
  103.3 86.7 %all-gather.2.cloned.1.call-start = ((), (), s32[]{:S(2)}) async-start(), calls=%async_computation.2 | async-start | bytes 2621440 | tf_op jit(solution)/shard_map/all_gather | solution.py:81
  104.0 225.0 %reduce-scatter.2.cloned.1.call-start = ((), (), s32[]{:S(2)}) async-start(), calls=%async_computation.3 | async-start | bytes 294912 | tf_op jit(solution)/shard_map/reduce_scatter | solution.py:146
  296.0 34.4 %copy-start.1 = (bf16[128,2048]{1,0:T(8,128)(2,1)S(1)}, bf16[128,2048]{1,0:T(8,128)(2,1)}, u32[]{:S(2)}) copy-start(bf16[128,2048]{1,0:T(8,128)(2,1)} %param.23) | copy-start | bytes 1572868
  (2 other events, 1.5 us)
Sparse Core Ops, SparseCore 0:
  105.6 74.5 all-gather.1
  298.0 30.9 reduce-scatter.1
